TPU v7x, 32 devices: a whole 2x2x4 slice. The times are simulated.
32 devices in a mesh: tm: 16 (over z, y, x), dp: 2 (over core).
Axes of the slice: x: 2, y: 2, z: 4, core: 2. Of those that a mesh axis runs over, the one named last changes fastest.
Arguments:
- state_feats: bfloat16 [128, 64, 256], P('dp', 'tm'), may hold values from -6 to 6
- achieved: bfloat16 [128, 64, 512], P('dp', 'tm'), may hold values from -6 to 6
- offsets: int32 [128, 64], P('dp', 'tm'), may hold values from 0 to 63, as said below
- w_in: bfloat16 [768, 2048], replicated, may hold values from -0.21875 to 0.21875
- b_in: float32 [2048], replicated, may hold values from -3 to 3
- w_out: float32 [2048], replicated, may hold values from -0.75 to 0.75
- b_out: float32 [1], replicated, may hold values from -1 to 1
Outputs:
- td_error: float32 [128, 64], P('dp', 'tm')
- grad_w_in: float32 [768, 2048], P(('tm', 'dp'))
- grad_b_in: float32 [2048], replicated
- grad_w_out: float32 [2048], replicated
- grad_b_out: float32 [1], replicated
Inputs may be any that keep to these rules, and one draw needn't show every extreme that they name: t + offsets[e, t] <= 63. The transitions held by one device (one index of dp and of tm) ask at most 4 of their goals from any other single index of tm; every device whose tm index is below the last asks exactly 4 goals from the last index, all of them at time 64 - 1.
All inputs are finite; a program needn't handle non-finite values.
Results may differ from a plain program's by a relative error of at most 0.0024.
The roundings to bfloat16 on the way count: a program that leaves them out, or rounds other values in their place, can miss the bound.
Values may be sent and summed in bfloat16 or wider, within the bound.
A program may use at most 64 MiB of HBM per device.

v0:
```python
import math

import jax
import jax.numpy as jnp
from jax import lax
from jax.sharding import PartitionSpec as P

CAP = 4


def body(state_feats, achieved, offsets, w_in, b_in, w_out, b_out):
    ep_dev, steps, goal_width = achieved.shape
    feat_width = state_feats.shape[2]
    rows = ep_dev * steps
    tm_count = lax.axis_size("tm")
    dp_count = lax.axis_size("dp")
    myself = lax.axis_index("tm")
    capacity = CAP
    times = myself * steps + jnp.arange(steps, dtype=jnp.int32)
    target = times[None, :] + offsets
    owner = (target // steps).reshape(rows)
    episode = jnp.broadcast_to(jnp.arange(ep_dev, dtype=jnp.int32)[:, None], (ep_dev, steps))
    position = (episode * steps + target % steps).reshape(rows)
    table = achieved.reshape(rows, goal_width)
    remote = owner != myself
    peers = jnp.arange(tm_count, dtype=jnp.int32)
    hits = ((owner[:, None] == peers[None, :]) & remote[:, None]).astype(jnp.int32)
    slot = jnp.sum((jnp.cumsum(hits, axis=0) - 1) * hits, axis=1)
    dest = jnp.where(remote, owner, tm_count)
    requests = (
        jnp.full((tm_count, capacity), -1, jnp.int32).at[dest, slot].set(position, mode="drop")
    )
    asked = lax.all_to_all(requests, "tm", split_axis=0, concat_axis=0, tiled=True)
    picked = jnp.take(table, jnp.clip(asked, 0, rows - 1), axis=0)
    picked = jnp.where((asked >= 0)[..., None], picked, jnp.zeros((), jnp.bfloat16))
    fetched = lax.all_to_all(picked, "tm", split_axis=0, concat_axis=0, tiled=True)
    fetched = fetched.reshape(tm_count * capacity, goal_width)
    far_rows = jnp.take(
        fetched, jnp.clip(owner * capacity + slot, 0, tm_count * capacity - 1), axis=0
    )
    near_rows = jnp.take(table, position, axis=0)
    goal = jnp.where(remote[:, None], far_rows, near_rows)
    inputs = jnp.concatenate([state_feats.reshape(rows, feat_width), goal], axis=1)
    pre = jnp.dot(inputs, w_in, preferred_element_type=jnp.float32) + b_in
    hidden = jax.nn.silu(pre).astype(jnp.bfloat16)
    hidden_wide = hidden.astype(jnp.float32)
    value = jnp.dot(hidden_wide, w_out, precision=lax.Precision.HIGHEST) + b_out[0]
    diff = table.astype(jnp.float32) - goal.astype(jnp.float32)
    reward = -jnp.mean(diff * diff, axis=1)
    error = value - reward
    scale = 1.0 / math.sqrt(rows * tm_count * dp_count)
    grad_value = error * scale
    sig = jax.nn.sigmoid(pre)
    grad_pre = grad_value[:, None] * w_out[None, :] * (sig * (1.0 + pre * (1.0 - sig)))
    grad_low = grad_pre.astype(jnp.bfloat16)
    small = (
        jnp.sum(grad_pre, axis=0),
        jnp.dot(grad_value, hidden_wide, precision=lax.Precision.HIGHEST),
        jnp.sum(grad_value, keepdims=True),
    )
    grad_b_in, grad_w_out, grad_b_out = lax.psum((small[0], small[1], small[2]), ("tm", "dp"))
    grad_w_in = lax.psum_scatter(
        lax.dot_general(
            inputs, grad_low, (((0,), (0,)), ((), ())), preferred_element_type=jnp.float32
        ),
        ("tm", "dp"),
        scatter_dimension=0,
        tiled=True,
    )
    return (error.reshape(ep_dev, steps), grad_w_in, grad_b_in, grad_w_out, grad_b_out)


def solution(mesh):
    in_specs = (P("dp", "tm", None), P("dp", "tm", None), P("dp", "tm"), P(), P(), P(), P())
    out_specs = (P("dp", "tm"), P(("tm", "dp"), None), P(), P(), P())
    return jax.shard_map(body, mesh=mesh, in_specs=in_specs, out_specs=out_specs, check_vma=False)
```

profile of v0, /device:TPU:0, one launch (start us, length us, event | category | flops | bytes accessed | tf_op | source)
XLA Modules:
  0.0 193.6 jit_solution(5366446118225717900)
XLA Ops:
  7.2 1.4 broadcast_compare_fusion
  11.0 11.3 %scatter_fusion = s32[16,4]{0,1:T(4,128)S(1)} fusion(s32[16,4]{0,1:T(4,128)S(1)} %broadcast_in_dim.84, s32[256]{0:T(256)S(1)} %bitcast.43, s32[256]{0:T(256)S(1)} %reshape.273), kind=kCustom, calls=%fused_computation.3 | custom fusion | bytes 5120 | tf_op jit(solution)/shard_map/scatter | solution.py:31
  22.4 0.7 copy.39
  23.1 8.4 %all-to-all-start = ((s32[16,1,4]{2,1,0:T(1,128)}), s32[16,1,4]{2,1,0:T(1,128)S(1)}, u32[]{:S(2)}, u32[]{:S(2)}) async-start(s32[16,1,4]{2,1,0:T(1,128)} %copy.39), calls=%async_computation | async-start | bytes 16384 | tf_op jit(solution)/shard_map/all_to_all | solution.py:33
  31.4 0.6 compare_and_fusion.2
  32.3 1.0 reshape.243
  33.4 5.3 %all-to-all-done = s32[16,1,4]{2,1,0:T(1,128)S(1)} async-done(((s32[16,1,4]{2,1,0:T(1,128)}), s32[16,1,4]{2,1,0:T(1,128)S(1)}, u32[]{:S(2)}, u32[]{:S(2)}) %all-to-all-start) | async-done | bytes 288 | tf_op jit(solution)/shard_map/all_to_all | solution.py:33
  39.0 0.7 gather_fusion
  39.9 0.7 select_select_fusion.1
  40.6 3.5 %all-to-all-start.1 = ((bf16[16,4,512]{2,1,0:T(4,128)(2,1)}), bf16[16,4,512]{2,1,0:T(4,128)(2,1)S(1)}, u32[]{:S(2)}, u32[]{:S(2)}) async-start(bf16[16,4,512]{2,1,0:T(4,128)(2,1)} %select_select_fusion.1), calls=%async_computation.1 | async-start | bytes 131072 | tf_op jit(solution)/shard_map/all_to_all | solution.py:36
  44.2 1.9 gather_fusion.2
  46.0 1.6 reshape.238
  47.7 1.7 gather.20
  49.5 0.8 copy.46
  50.3 1.4 copy.49
  52.3 1.3 pad_clamp_fusion.1
  53.6 2.0 %gather_fusion.1 = bf16[256,512]{1,0:T(8,128)(2,1)} fusion(bf16[64,512]{1,0:T(8,128)(2,1)S(1)} %reshape.244, s32[1024]{0:T(1024)} %pad_clamp_fusion.1), kind=kCustom, calls=%fused_computation.1 | custom fusion | bytes 525312 | tf_op jit(solution)/shard_map/jit(_take)/gather | solution.py:38
  55.6 1.8 gather.19
  57.3 1.7 multiply_reduce_fusion
  59.0 0.6 multiply_negate_fusion
  59.6 0.9 neg.13
  60.5 1.1 select_select_fusion
  61.7 1.9 %multiply_convert_fusion = (bf16[256,2048]{1,0:T(8,128)(2,1)S(1)}, f32[256,2048]{1,0:T(8,128)S(1)}) fusion(f32[2048]{0:T(1024)} %param.11, bf16[768,2048]{1,0:T(8,128)(2,1)S(1)} %copy-done, bf16[256,512]{1,0:T(8,128)(2,1)S(1)} %select_select_fusion, bf16[256,256]{1,0:T(8,128)(2,1)S(1)} %copy-done.4), kind=kOutput, calls=%fused_computation.6 | convolution fusion | flops 809238528 | bytes 6692864 | tf_op jit(solution)/shard_map/dot_general | solution.py:44
  63.6 1.0 copy-done.1
  64.7 0.9 fusion.15
  65.6 0.7 fusion.12
  66.3 4.0 %fusion = f32[768,2048]{1,0:T(8,128)} fusion(bf16[256,512]{1,0:T(8,128)(2,1)S(1)} %select_select_fusion, bf16[256,256]{1,0:T(8,128)(2,1)S(1)} %copy-done.4, f32[256,2048]{1,0:T(8,128)S(1)} %get-tuple-element.34, f32[2048]{0:T(1024)S(1)} %copy-done.5, f32[256]{0:T(256)S(1)} %broadcast_multiply_fusion), kind=kOutput, calls=%fused_computation.8 | convolution fusion | flops 811335680 | bytes 8791040 | tf_op jit(solution)/shard_map/dot_general | solution.py:63
  70.4 0.7 copy.50
  71.1 1.7 fusion.16
  72.8 2.4 %fusion.13 = f32[2048]{0:T(1024)S(1)} fusion(f32[256,2048]{1,0:T(8,128)} %copy-done.3, f32[2048]{0:T(1024)S(1)} %copy-done.5, f32[256]{0:T(256)S(1)} %broadcast_multiply_fusion), kind=kLoop, calls=%fused_computation.69 | loop fusion | flops 5240832 | bytes 2114560 | tf_op jit(solution)/shard_map/reduce_sum | solution.py:57
  75.3 41.1 %all-reduce = (f32[2048]{0:T(1024)}, f32[2048]{0:T(1024)}, f32[1]{0:T(128)}) all-reduce(f32[2048]{0:T(1024)S(1)} %fusion.13, f32[2048]{0:T(1024)S(1)} %bitcast.45, f32[1]{0:T(128)} %bitcast.14), channel_id=1, replica_groups=mesh['tm'=16,'dp'=2] {'tm','dp'}, use_global_device_ids=true, to_apply=%region_7.8 | all-reduce | flops 4097 | bytes 32776 | tf_op jit(solution)/shard_map/psum | solution.py:61
  116.3 70.4 %reduce-scatter.2.cloned.1.call-done = f32[24,2048]{1,0:T(8,128)} async-done(((f32[768,2048]{1,0:T(8,128)}), f32[24,2048]{1,0:T(8,128)}) %reduce-scatter.2.cloned.1.call-update) | async-done | bytes 196624 | tf_op jit(solution)/shard_map/reduce_scatter | solution.py:62
  (54 shorter events, 3.5 us)
Async XLA Ops:
  7.2 54.5 %copy-start = (bf16[768,2048]{1,0:T(8,128)(2,1)S(1)}, bf16[768,2048]{1,0:T(8,128)(2,1)}, u32[]{:S(2)}) copy-start(bf16[768,2048]{1,0:T(8,128)(2,1)} %param.10) | copy-start | bytes 9437188
  9.9 0.5 copy-start.6
  23.1 15.6 %all-to-all-start = ((s32[16,1,4]{2,1,0:T(1,128)}), s32[16,1,4]{2,1,0:T(1,128)S(1)}, u32[]{:S(2)}, u32[]{:S(2)}) async-start(s32[16,1,4]{2,1,0:T(1,128)} %copy.39), calls=%async_computation | async-start | bytes 16384 | tf_op jit(solution)/shard_map/all_to_all | solution.py:33
  40.6 12.9 %all-to-all-start.1 = ((bf16[16,4,512]{2,1,0:T(4,128)(2,1)}), bf16[16,4,512]{2,1,0:T(4,128)(2,1)S(1)}, u32[]{:S(2)}, u32[]{:S(2)}) async-start(bf16[16,4,512]{2,1,0:T(4,128)(2,1)} %select_select_fusion.1), calls=%async_computation.1 | async-start | bytes 131072 | tf_op jit(solution)/shard_map/all_to_all | solution.py:36
  44.1 142.6 %reduce-scatter.2.cloned.1.call-start = ((), (), s32[]{:S(2)}) async-start(), calls=%async_computation.3 | async-start | bytes 6488064 | tf_op jit(solution)/shard_map/reduce_scatter | solution.py:62
  49.5 11.0 %copy-start.2 = (bf16[256,512]{1,0:T(8,128)(2,1)S(1)}, bf16[256,512]{1,0:T(8,128)(2,1)}, u32[]{:S(2)}) copy-start(bf16[256,512]{1,0:T(8,128)(2,1)} %gather_fusion.2) | copy-start | bytes 786436
  55.6 6.1 %copy-start.4 = (bf16[256,256]{1,0:T(8,128)(2,1)S(1)}, bf16[256,256]{1,0:T(8,128)(2,1)}, u32[]{:S(2)}) copy-start(bf16[256,256]{1,0:T(8,128)(2,1)} %reshape.238) | copy-start | bytes 393220
  61.7 3.0 %copy-start.5 = (f32[2048]{0:T(1024)S(1)}, f32[2048]{0:T(1024)}, u32[]{:S(2)}) copy-start(f32[2048]{0:T(1024)} %param.12) | copy-start | bytes 24580
  63.6 1.1 copy-start.1
  63.6 2.7 %copy-start.3 = (f32[256,2048]{1,0:T(8,128)}, f32[256,2048]{1,0:T(8,128)S(1)}, u32[]{:S(2)}) copy-start(f32[256,2048]{1,0:T(8,128)S(1)} %get-tuple-element.34) | copy-start | bytes 6291460
Sparse Core Ops, SparseCore 0:
  70.4 116.2 reduce-scatter.1
where the time goes:
time: 194 us
  waiting for transfers between devices  75.7 us (39%)
  blocking collectives  41.1 us (21%)
  local copies, waits for them, and re-layouts  29.4 us (15%)
  between operations  14.9 us (8%)
  other arithmetic  12 us (6%)
  starting transfers between devices  11.9 us (6%)
  matrix products  8.6 us (4%)
    reduce_scatter x1, waiting for transfers between devices, body(): lax.psum_scatter(lax.dot_general(inputs, grad_low, (((0,), (0,)), ((), ()...  70.4 us
    psum x1, blocking collectives, body(): lax.psum((small[0], small[1], small[2]), ('tm', 'dp'))  41.1 us
    scatter x1, local copies, waits for them, and re-layouts, body(): jnp.full((tm_count, capacity), -1, jnp.int32).at[dest, slot]  11.3 us
    all_to_all x1, starting transfers between devices, body(): lax.all_to_all(requests, 'tm', split_axis=0, concat_axis=0, tiled=True)  8.37 us
    all_to_all x1, waiting for transfers between devices, body(): lax.all_to_all(requests, 'tm', split_axis=0, concat_axis=0, tiled=True)  5.28 us
    dot_general x1, matrix products, body(): lax.dot_general(inputs, grad_low, (((0,), (0,)), ((), ())), preferred_ele...  4.01 us
  transfers between devices with their start and end apart: 3, of which 2 were waited for; matrix products, arithmetic and copies ran while one was open for 8% of the time, Pallas kernels for 0%

commit v1 on v0

v1 whole, which is shorter than its diff:
```python
import functools
import math

import jax
import jax.numpy as jnp
from jax import lax
from jax.experimental import pallas as pl
from jax.experimental.pallas import tpu as pltpu
from jax.sharding import PartitionSpec as P

CAP = 4
LANES = 128
GROUP = 8
MESH = pl.DeviceIdType.MESH
BF16 = jnp.bfloat16
F32 = jnp.float32


def iota(shape, axis):
    return lax.broadcasted_iota(jnp.int32, shape, axis)


def dot(a, b):
    return jnp.dot(a, b, preferred_element_type=F32)


def dot_rows(a, b):
    return lax.dot_general(a, b, (((0,), (0,)), ((), ())), preferred_element_type=F32)


def onehot(mask):
    return jnp.where(mask, 1.0, 0.0).astype(BF16)


def wait_bytes(ref, sem):
    pltpu.make_async_copy(ref, ref, sem).wait()


def kernel(dims, sf_ref, ach_ref, off_ref, w_hbm, b_ref, wo_ref, bo_ref,
           err_ref, gw_ref, gb_ref, gwo_ref, gbo_ref,
           w, pre, hid, low, low_send, xt, req_send, req_recv, resp_send, resp_recv,
           big_send, big_recv, own, sm_send, sm_recv, all_send, all_recv,
           w_sem, pair_send, pair_recv, s_sem, r_sem):
    tm_n, dp_n, steps, rdev, rpad = dims
    n = tm_n * dp_n
    rows, feat = sf_ref.shape
    goal_w = ach_ref.shape[1]
    hidden_n = wo_ref.shape[1]
    half = hidden_n // dp_n
    inner = feat + goal_w
    nc = goal_w // LANES
    slots = CAP * nc
    peers = tm_n - 1
    tm = lax.axis_index("tm")
    dp = lax.axis_index("dp")
    me = tm * dp_n + dp
    partner = (tm, 1 - dp)

    w_copy = pltpu.make_async_copy(w_hbm, w, w_sem)
    w_copy.start()

    barrier = pltpu.get_barrier_semaphore()

    def greet(k, c):
        dev = lax.rem(me + k, n)
        pl.semaphore_signal(barrier, inc=1, device_id=(dev // dp_n, lax.rem(dev, dp_n)), device_id_type=MESH)
        return c

    lax.fori_loop(1, n, greet, 0)

    def remote(src, dst, ss, rs, dev):
        return pltpu.make_async_remote_copy(
            src_ref=src, dst_ref=dst, send_sem=ss, recv_sem=rs, device_id=dev, device_id_type=MESH)

    r = iota((1, rows), 1)
    ahead = lax.rem(r, steps) + off_ref[...]
    rel = ahead // steps
    pos = (r // steps) * steps + lax.rem(ahead, steps)
    i = iota((peers * slots, rows), 0)
    hits = (i // slots + 1) == rel
    tri = onehot(iota((rows, rows), 0) <= iota((rows, rows), 1))
    rank = dot(onehot(hits), tri).astype(jnp.int32)
    sel = hits & (rank == lax.rem(i, CAP) + 1)
    want = jnp.sum(jnp.where(sel, pos + 1, 0).astype(F32), axis=1, keepdims=True) - 1.0
    req_send[...] = jnp.broadcast_to(want, (peers * slots, LANES)).astype(BF16).reshape(peers, slots, LANES)

    pl.semaphore_wait(barrier, n - 1)

    def ask(k, c):
        remote(req_send.at[k - 1], req_recv.at[k - 1], s_sem.at[0], r_sem.at[0],
               (lax.rem(tm + k, tm_n), dp)).start()
        return c

    lax.fori_loop(1, tm_n, ask, 0)

    table = ach_ref[...]
    near = onehot((iota((rows, rows), 0) == pos) & (rel == 0))
    goal_near = dot_rows(near, table)
    sf = sf_ref[...]
    if rpad == rdev:
        xt[0, 0:feat, :] = sf.T
    w_copy.wait()
    cw = 256
    chunks = hidden_n // cw

    def first(j, c):
        cols = pl.ds(pl.multiple_of(j * cw, cw), cw)
        pre[:, cols] = dot(sf, w[0:feat, cols]) + b_ref[:, cols]
        return c

    wait_bytes(req_recv, r_sem.at[0])
    asked = req_recv[...].reshape(peers * slots, LANES).astype(F32)
    asked = jnp.concatenate([asked] * (rows // LANES), axis=1).astype(jnp.int32)
    found = asked == iota((peers * slots, rows), 1)
    part = lax.rem(i, slots) // CAP
    picked = jnp.zeros((peers * slots, LANES), F32)
    for c in range(nc):
        picked = picked + dot(onehot(found & (part == c)), table[:, c * LANES:(c + 1) * LANES])
    resp_send[...] = picked.astype(BF16).reshape(peers, slots, LANES)

    def answer(k, c):
        remote(resp_send.at[k - 1], resp_recv.at[k - 1], s_sem.at[1], r_sem.at[1],
               (lax.rem(tm - k + tm_n, tm_n), dp)).start()
        return c

    lax.fori_loop(1, tm_n, answer, 0)
    lax.fori_loop(0, chunks, first, 0)
    wait_bytes(resp_recv, r_sem.at[1])
    fetched = resp_recv[...].reshape(peers * slots, LANES)
    far = [dot_rows(onehot(sel & (part == c)), fetched) for c in range(nc)]
    goal_wide = goal_near + jnp.concatenate(far, axis=1)
    goal = goal_wide.astype(BF16)

    if rpad == rdev:
        xt[0, feat:inner, :] = goal.T
    else:
        x = jnp.concatenate([sf, goal], axis=1)
        o = iota((n * rpad, inner), 0)
        place = (o // rpad) * rdev + lax.rem(o, rpad)
        place = jnp.where(lax.rem(o, rpad) < rdev, place, -1)
        xt[0] = lax.dot_general(onehot(place == iota((n * rpad, inner), 1)), x,
                                (((1,), (1,)), ((), ())), preferred_element_type=F32).astype(BF16)
    x_copy = remote(xt.at[0], xt.at[1], pair_send.at[0], pair_recv.at[0], partner)
    x_copy.start()

    diff = table.astype(F32) - goal_wide
    reward = -jnp.mean(diff * diff, axis=1, keepdims=True)

    def second(j, acc):
        cols = pl.ds(pl.multiple_of(j * cw, cw), cw)
        p = pre[:, cols] + dot(goal, w[feat:inner, cols])
        s = 1.0 / (1.0 + jnp.exp(-p))
        wo = wo_ref[:, cols]
        h = (p * s).astype(BF16)
        hid[:, cols] = h
        pre[:, cols] = wo * (s * (1.0 + p * (1.0 - s)))
        v = h.astype(F32) * wo
        for q in range(cw // LANES):
            acc = acc + v[:, q * LANES:(q + 1) * LANES]
        return acc

    acc = lax.fori_loop(0, chunks, second, jnp.zeros((rows, LANES), F32))
    value = jnp.sum(acc, axis=1, keepdims=True) + bo_ref[...]
    error = value - reward
    diag = iota((rows, rows), 0) == iota((rows, rows), 1)
    err_ref[...] = jnp.sum(jnp.where(diag, error, 0.0), axis=0, keepdims=True)
    gv = error * (1.0 / math.sqrt(rows * n))
    gbo = jnp.broadcast_to(jnp.sum(gv, axis=0, keepdims=True), (1, LANES))

    per = cw // LANES
    hv = hidden_n // LANES

    def back(which, out):
        def step(j, c):
            col = pl.multiple_of(which * half + j * cw, cw)
            cols = pl.ds(col, cw)
            g = gv * pre[:, cols]
            out[:, pl.ds(pl.multiple_of(j * cw, cw), cw)] = g.astype(BF16)
            gs = jnp.sum(g, axis=0, keepdims=True)
            hs = jnp.sum(gv * hid[:, cols].astype(F32), axis=0, keepdims=True)
            at = which * (half // LANES) + j * per
            for q in range(per):
                lanes = slice(q * LANES, (q + 1) * LANES)
                sm_send[at + q] = jnp.concatenate([gs[:, lanes], gbo], axis=1)
                sm_send[hv + at + q] = jnp.concatenate([hs[:, lanes], gbo], axis=1)
            return c
        return step

    lax.fori_loop(0, half // cw, back(1 - dp, low_send), 0)
    l_copy = remote(low_send, low.at[1], pair_send.at[1], pair_recv.at[1], partner)
    l_copy.start()
    lax.fori_loop(0, half // cw, back(dp, low.at[0]), 0)

    owners = 2 * hv

    def small(k, c):
        dev = lax.rem(me + k, n)

        def go():
            remote(sm_send.at[dev], sm_recv.at[k - 1], s_sem.at[2], r_sem.at[2],
                   (dev // dp_n, lax.rem(dev, dp_n))).start()
        if owners == n:
            go()
        else:
            pl.when(dev < owners)(go)
        return c

    lax.fori_loop(1, n, small, 0)
    x_copy.wait_recv()
    l_copy.wait_recv()

    block = GROUP * rpad
    groups = n // GROUP

    def form(g, c):
        base = lax.rem(me // GROUP + 1 + g, groups)
        at = pl.ds(pl.multiple_of(base * block, block), block)
        p = dot(xt[0, at, :], low[0]) + dot(xt[1, at, :], low[1])
        for d in range(GROUP):
            dev = base * GROUP + d
            blk = p[d * rpad:(d + 1) * rpad]
            blk = jnp.concatenate([blk[:, :half // 2], blk[:, half // 2:]], axis=0)
            big_send[dev] = blk.astype(BF16)

            @pl.when(dev == me)
            def _():
                own[...] = blk

            @pl.when(dev != me)
            def _():
                k = lax.rem(dev - me + n, n)
                remote(big_send.at[dev], big_recv.at[k - 1], s_sem.at[3], r_sem.at[3],
                       (dev // dp_n, lax.rem(dev, dp_n))).start()
        return c

    lax.fori_loop(0, groups, form, 0)

    def total():
        wait_bytes(sm_recv, r_sem.at[2])
        all_send[...] = sm_send[me] + jnp.sum(sm_recv[...], axis=0)
        all_recv[me] = all_send[...]

        def tell(k, c):
            dev = lax.rem(me + k, n)
            remote(all_send, all_recv.at[me], s_sem.at[4], r_sem.at[4],
                   (dev // dp_n, lax.rem(dev, dp_n))).start()
            return c

        lax.fori_loop(1, n, tell, 0)

    if owners == n:
        total()
        wait_bytes(all_recv.at[pl.ds(0, n - 1)], r_sem.at[4])
    else:
        pl.when(me < owners)(total)

        @pl.when(me < owners)
        def _():
            wait_bytes(all_recv.at[pl.ds(0, owners - 1)], r_sem.at[4])

        @pl.when(me >= owners)
        def _():
            wait_bytes(all_recv.at[pl.ds(0, owners)], r_sem.at[4])
    for q in range(hv):
        lanes = slice(q * LANES, (q + 1) * LANES)
        gb_ref[:, lanes] = all_recv[q][:, :LANES]
        gwo_ref[:, lanes] = all_recv[hv + q][:, :LANES]
    gbo_ref[...] = all_recv[0][:, LANES:LANES + 1]

    wait_bytes(big_recv, r_sem.at[3])

    def add(k, c):
        same, other = c
        return same + big_recv[2 * k + 1].astype(F32), other + big_recv[2 * k].astype(F32)

    q4 = half // 4
    for q in range(2):
        lanes = slice(q * q4, (q + 1) * q4)

        def add(k, c):
            same, other = c
            return (same + big_recv[2 * k + 1, :, lanes].astype(F32),
                    other + big_recv[2 * k, :, lanes].astype(F32))

        same, other = lax.fori_loop(
            0, tm_n - 1, add, (own[:, lanes], jnp.zeros((2 * rpad, q4), F32)))
        other = other + big_recv[n - 2, :, lanes].astype(F32)
        for which, val in ((dp, same), (1 - dp, other)):
            for z in range(2):
                col = pl.multiple_of(which * half + z * (half // 2) + q * q4, LANES)
                gw_ref[:, pl.ds(col, q4)] = val[z * rpad:z * rpad + rdev]

    wait_bytes(req_send, s_sem.at[0])
    wait_bytes(resp_send, s_sem.at[1])
    x_copy.wait_send()
    l_copy.wait_send()
    if owners == n:
        wait_bytes(sm_send.at[pl.ds(0, n - 1)], s_sem.at[2])
        wait_bytes(all_recv.at[pl.ds(0, n - 1)], s_sem.at[4])
    else:
        @pl.when(me < owners)
        def _():
            wait_bytes(sm_send.at[pl.ds(0, owners - 1)], s_sem.at[2])
            wait_bytes(sm_recv, s_sem.at[4])

        @pl.when(me >= owners)
        def _():
            wait_bytes(sm_send.at[pl.ds(0, owners)], s_sem.at[2])
    wait_bytes(big_send.at[pl.ds(0, n - 1)], s_sem.at[3])


def body(tm_n, dp_n, state_feats, achieved, offsets, w_in, b_in, w_out, b_out):
    ep_dev, steps, goal_w = achieved.shape
    feat = state_feats.shape[2]
    rows = ep_dev * steps
    inner, hidden_n = w_in.shape
    n = tm_n * dp_n
    half = hidden_n // dp_n
    rdev = inner // n
    rpad = -(-rdev // 8) * 8
    slots = CAP * (goal_w // LANES)
    owners = 2 * hidden_n // LANES
    assert dp_n == 2 and rows <= 256 and owners <= n and n % GROUP == 0
    vmem = pl.BlockSpec(memory_space=pltpu.VMEM)
    out = pl.pallas_call(
        functools.partial(kernel, (tm_n, dp_n, steps, rdev, rpad)),
        out_shape=(
            jax.ShapeDtypeStruct((1, rows), F32),
            jax.ShapeDtypeStruct((rdev, hidden_n), F32),
            jax.ShapeDtypeStruct((1, hidden_n), F32),
            jax.ShapeDtypeStruct((1, hidden_n), F32),
            jax.ShapeDtypeStruct((1, 1), F32),
        ),
        in_specs=[vmem] * 3 + [pl.BlockSpec(memory_space=pl.ANY)] + [vmem] * 3,
        out_specs=[vmem] * 5,
        scratch_shapes=[
            pltpu.VMEM((inner, hidden_n), BF16),
            pltpu.VMEM((rows, hidden_n), F32),
            pltpu.VMEM((rows, hidden_n), BF16),
            pltpu.VMEM((2, rows, half), BF16),
            pltpu.VMEM((rows, half), BF16),
            pltpu.VMEM((2, n * rpad, rows), BF16),
            pltpu.VMEM((tm_n - 1, slots, LANES), BF16),
            pltpu.VMEM((tm_n - 1, slots, LANES), BF16),
            pltpu.VMEM((tm_n - 1, slots, LANES), BF16),
            pltpu.VMEM((tm_n - 1, slots, LANES), BF16),
            pltpu.VMEM((n, 2 * rpad, half // 2), BF16),
            pltpu.VMEM((n - 1, 2 * rpad, half // 2), BF16),
            pltpu.VMEM((2 * rpad, half // 2), F32),
            pltpu.VMEM((owners, 1, 2 * LANES), F32),
            pltpu.VMEM((n - 1, 1, 2 * LANES), F32),
            pltpu.VMEM((1, 2 * LANES), F32),
            pltpu.VMEM((owners, 1, 2 * LANES), F32),
            pltpu.SemaphoreType.DMA,
            pltpu.SemaphoreType.DMA((2,)),
            pltpu.SemaphoreType.DMA((2,)),
            pltpu.SemaphoreType.DMA((5,)),
            pltpu.SemaphoreType.DMA((5,)),
        ],
        compiler_params=pltpu.CompilerParams(
            collective_id=0, has_side_effects=True, vmem_limit_bytes=60 * 1024 * 1024),
    )(state_feats.reshape(rows, feat), achieved.reshape(rows, goal_w), offsets.reshape(1, rows),
      w_in, b_in.reshape(1, hidden_n), w_out.reshape(1, hidden_n), b_out.reshape(1, 1))
    err, gw, gb, gwo, gbo = out
    return (err.reshape(ep_dev, steps), gw, gb.reshape(hidden_n), gwo.reshape(hidden_n), gbo.reshape(1))


def solution(mesh):
    in_specs = (P("dp", "tm", None), P("dp", "tm", None), P("dp", "tm"), P(), P(), P(), P())
    out_specs = (P("dp", "tm"), P(("tm", "dp"), None), P(), P(), P())
    step = functools.partial(body, mesh.shape["tm"], mesh.shape["dp"])
    return jax.shard_map(step, mesh=mesh, in_specs=in_specs, out_specs=out_specs, check_vma=False)
```

time: 194 us -> 78.7 us (0.41)
  waiting for transfers between devices: 75.7 us -> 0 us
  Pallas kernels: 0 us -> 63.7 us
  blocking collectives: 41.1 us -> 0 us
  local copies, waits for them, and re-layouts: 29.4 us -> 10.2 us
  starting transfers between devices: 11.9 us -> 0 us
  between operations: 14.9 us -> 3.04 us
  other arithmetic: 12 us -> 1.32 us
  matrix products: 8.6 us -> 0 us
    reduce_scatter x1 -> x0, waiting for transfers between devices: 70.4 us -> none  [body(): lax.psum_scatter(lax.dot_general(inputs, grad_low, (((0,), (0,)), ((), ()...]
    pallas_call x0 -> x1, Pallas kernels: none -> 63.7 us  [body(): pl.pallas_call(functools.partial(kernel, (tm_n, dp_n, steps, rdev, rpad))...]
    psum x1 -> x0, blocking collectives: 41.1 us -> none  [body(): lax.psum((small[0], small[1], small[2]), ('tm', 'dp'))]
    all_to_all x2 -> x0, starting transfers between devices: 11.9 us -> none  [the longest x1 8.37 us: body(): lax.all_to_all(requests, 'tm', split_axis=0, concat_axis=0, tiled=True)]
    scatter x1 -> x0, local copies, waits for them, and re-layouts: 11.3 us -> none  [body(): jnp.full((tm_count, capacity), -1, jnp.int32).at[dest, slot]]
    dot_general x4 -> x0, matrix products: 8.6 us -> none  [the longest x1 4.01 us: body(): lax.dot_general(inputs, grad_low, (((0,), (0,)), ((), ())), preferred_ele...]
    gather x6 -> x0, local copies, waits for them, and re-layouts: 8.04 us -> none  [the longest x2 3.74 us: body(): jnp.take(fetched, jnp.clip(owner * capacity + slot, 0, tm_count * capacit...]
    all_to_all x2 -> x0, waiting for transfers between devices: 5.29 us -> none  [the longest x1 5.28 us: body(): lax.all_to_all(requests, 'tm', split_axis=0, concat_axis=0, tiled=True)]
  transfers between devices with their start and end apart: 3 -> 0, of which waited for: 2 -> 0; matrix products, arithmetic and copies ran while one was open for 8% -> 0% of each run, Pallas kernels for 0% -> 0%
where the time goes in v1:
time: 78.7 us; the launch traced here: 78.3 us
  Pallas kernels  63.7 us (81%)
  local copies, waits for them, and re-layouts  10.2 us (13%)
  between operations  3.04 us (4%)
  other arithmetic  1.32 us (2%)
    pallas_call x1, Pallas kernels, body(): pl.pallas_call(functools.partial(kernel, (tm_n, dp_n, steps, rdev, rpad))...  63.7 us
    unnamed x5, local copies, waits for them, and re-layouts  5.63 us
    reshape x1, local copies, waits for them, and re-layouts, body(): achieved.reshape(rows, goal_w)  1.71 us
    reshape x1, local copies, waits for them, and re-layouts, body(): state_feats.reshape(rows, feat)  1.59 us

profile of v1, /device:TPU:0, one launch (start us, length us, event | category | flops | bytes accessed | tf_op | source)
XLA Modules:
  0.0 78.3 jit_solution(6956170839235514007)
XLA Ops:
  0.6 1.7 %reshape.41.ach_ref = bf16[256,512]{1,0:T(8,128)(2,1)} reshape(bf16[64,4,512]{2,1,0:T(4,128)(2,1)} %param.8) | data formatting | bytes 524288 | tf_op jit(solution)/shard_map/reshape | solution.py:362
  2.3 1.6 %reshape.40.sf_ref = bf16[256,256]{1,0:T(8,128)(2,1)} reshape(bf16[64,4,256]{2,1,0:T(4,128)(2,1)} %param.7) | data formatting | bytes 262144 | tf_op jit(solution)/shard_map/reshape | solution.py:362
  3.9 0.8 copy.14
  4.7 0.7 reshape.42.off_ref
  6.0 63.7 %shard_map.110 = (f32[1,256]{1,0:T(1,128)}, f32[24,2048]{1,0:T(8,128)}, f32[1,2048]{1,0:T(1,128)}, f32[1,2048]{1,0:T(1,128)}, f32[1,1]{1,0:T(1,128)}) custom-call(bf16[256,256]{1,0:T(8,128)(2,1)} %reshape.40.sf_ref, bf16[256,512]{1,0:T(8,128)(2,1)} %reshape.41.ach_ref, s32[1,256]{1,0:T(1,128)} %reshape.42.off_ref, bf16[768,2048]{1,0:T(8,128)(2,1)} %w_hbm.1, ...), custom_call_target="tpu_custom_call" | custom-call | tf_op jit(solution)/shard_map/pallas_call | solution.py:325
  69.8 0.5 broadcast.3
  70.3 1.3 %reduce.3 = f32[256]{0:T(256)S(1)} reduce(f32[1,256]{1,0:T(1,128)} %get-tuple-element.10, f32[]{:T(128)} %broadcast.3), dimensions={0}, to_apply=%get-tuple-element.10.reduce_sub_computation.3 | reduce | bytes 2052 | tf_op jit(solution)/shard_map/pallas_call | solution.py:325
  71.6 0.1 reshape.46
  71.7 0.7 copy.15
  72.4 1.6 %copy.21 = f32[24,2048]{1,0:T(8,128)} copy(f32[24,2048]{1,0:T(8,128)} %get-tuple-element.31) | data formatting | bytes 393216
  74.0 1.3 %copy.22 = f32[2048]{0:T(1024)} copy(f32[2048]{0:T(1024)} %bitcast.10) | data formatting | bytes 16384
  75.3 1.3 %copy.23 = f32[2048]{0:T(1024)} copy(f32[2048]{0:T(1024)} %bitcast.9) | data formatting | bytes 16384

commit v2 on v1

--- a/solution.py
+++ b/solution.py
@@ -36,15 +36,16 @@
     pltpu.make_async_copy(ref, ref, sem).wait()
 
 
-def kernel(dims, sf_ref, ach_ref, off_ref, w_hbm, b_ref, wo_ref, bo_ref,
+def kernel(dims, sf_hbm, ach_hbm, off_hbm, w_hbm, b_hbm, wo_hbm, bo_ref,
            err_ref, gw_ref, gb_ref, gwo_ref, gbo_ref,
-           w, pre, hid, low, low_send, xt, req_send, req_recv, resp_send, resp_recv,
+           sf_ref, ach_ref, off_ref, b_ref, wo_ref, w, pre, hid, low, low_send, xt, req_send, req_recv, resp_send, resp_recv,
            big_send, big_recv, own, sm_send, sm_recv, all_send, all_recv,
-           w_sem, pair_send, pair_recv, s_sem, r_sem):
+           in_sem, pair_send, pair_recv, s_sem, r_sem):
     tm_n, dp_n, steps, rdev, rpad = dims
     n = tm_n * dp_n
-    rows, feat = sf_ref.shape
-    goal_w = ach_ref.shape[1]
+    ep_dev, _, feat = sf_ref.shape
+    rows = ep_dev * steps
+    goal_w = ach_ref.shape[2]
     hidden_n = wo_ref.shape[1]
     half = hidden_n // dp_n
     inner = feat + goal_w
@@ -56,8 +57,11 @@
     me = tm * dp_n + dp
     partner = (tm, 1 - dp)
 
-    w_copy = pltpu.make_async_copy(w_hbm, w, w_sem)
-    w_copy.start()
+    loads = [pltpu.make_async_copy(src, dst, in_sem.at[j]) for j, (src, dst) in enumerate((
+        (off_hbm, off_ref), (ach_hbm, ach_ref), (sf_hbm, sf_ref), (b_hbm, b_ref), (wo_hbm, wo_ref),
+        (w_hbm, w)))]
+    for load in loads:
+        load.start()
 
     barrier = pltpu.get_barrier_semaphore()
 
@@ -72,8 +76,15 @@
         return pltpu.make_async_remote_copy(
             src_ref=src, dst_ref=dst, send_sem=ss, recv_sem=rs, device_id=dev, device_id_type=MESH)
 
+    loads[0].wait()
+
     r = iota((1, rows), 1)
-    ahead = lax.rem(r, steps) + off_ref[...]
+    spread = onehot(iota((ep_dev, rows), 0) == iota((ep_dev, rows), 1) // steps)
+    off = off_ref[...]
+    off = (dot((off // LANES).astype(F32).astype(BF16), spread) * LANES
+           + dot(lax.rem(off, LANES).astype(F32).astype(BF16), spread)).astype(jnp.int32)
+    off = jnp.sum(jnp.where(iota((steps, rows), 0) == lax.rem(r, steps), off, 0), axis=0, keepdims=True)
+    ahead = lax.rem(r, steps) + off
     rel = ahead // steps
     pos = (r // steps) * steps + lax.rem(ahead, steps)
     i = iota((peers * slots, rows), 0)
@@ -93,13 +104,16 @@
 
     lax.fori_loop(1, tm_n, ask, 0)
 
-    table = ach_ref[...]
+    loads[1].wait()
+    table = ach_ref[...].reshape(rows, goal_w)
     near = onehot((iota((rows, rows), 0) == pos) & (rel == 0))
     goal_near = dot_rows(near, table)
-    sf = sf_ref[...]
+    loads[2].wait()
+    sf = sf_ref[...].reshape(rows, feat)
     if rpad == rdev:
         xt[0, 0:feat, :] = sf.T
-    w_copy.wait()
+    for load in loads[3:]:
+        load.wait()
     cw = 256
     chunks = hidden_n // cw
 
@@ -160,10 +174,13 @@
         return acc
 
     acc = lax.fori_loop(0, chunks, second, jnp.zeros((rows, LANES), F32))
-    value = jnp.sum(acc, axis=1, keepdims=True) + bo_ref[...]
+    value = jnp.sum(acc, axis=1, keepdims=True) + bo_ref[0]
     error = value - reward
-    diag = iota((rows, rows), 0) == iota((rows, rows), 1)
-    err_ref[...] = jnp.sum(jnp.where(diag, error, 0.0), axis=0, keepdims=True)
+    er = iota((rows, ep_dev), 0)
+    home = er // steps == iota((rows, ep_dev), 1)
+    for t in range(steps):
+        err_ref[t:t + 1, :] = jnp.sum(
+            jnp.where(home & (lax.rem(er, steps) == t), error, 0.0), axis=0, keepdims=True)
     gv = error * (1.0 / math.sqrt(rows * n))
     gbo = jnp.broadcast_to(jnp.sum(gv, axis=0, keepdims=True), (1, LANES))
 
@@ -307,6 +324,11 @@
         def _():
             wait_bytes(sm_send.at[pl.ds(0, owners)], s_sem.at[2])
     wait_bytes(big_send.at[pl.ds(0, n - 1)], s_sem.at[3])
+
+
+def settle(*refs):
+    for src, dst in zip(refs[:5], refs[5:]):
+        dst[...] = src[...]
 
 
 def body(tm_n, dp_n, state_feats, achieved, offsets, w_in, b_in, w_out, b_out):
@@ -325,15 +347,20 @@
     out = pl.pallas_call(
         functools.partial(kernel, (tm_n, dp_n, steps, rdev, rpad)),
         out_shape=(
-            jax.ShapeDtypeStruct((1, rows), F32),
+            jax.ShapeDtypeStruct((steps, ep_dev), F32),
             jax.ShapeDtypeStruct((rdev, hidden_n), F32),
             jax.ShapeDtypeStruct((1, hidden_n), F32),
             jax.ShapeDtypeStruct((1, hidden_n), F32),
             jax.ShapeDtypeStruct((1, 1), F32),
         ),
-        in_specs=[vmem] * 3 + [pl.BlockSpec(memory_space=pl.ANY)] + [vmem] * 3,
+        in_specs=[pl.BlockSpec(memory_space=pltpu.HBM)] * 6 + [pl.BlockSpec(memory_space=pltpu.SMEM)],
         out_specs=[vmem] * 5,
         scratch_shapes=[
+            pltpu.VMEM((ep_dev, steps, feat), BF16),
+            pltpu.VMEM((ep_dev, steps, goal_w), BF16),
+            pltpu.VMEM((steps, ep_dev), jnp.int32),
+            pltpu.VMEM((1, hidden_n), F32),
+            pltpu.VMEM((1, hidden_n), F32),
             pltpu.VMEM((inner, hidden_n), BF16),
             pltpu.VMEM((rows, hidden_n), F32),
             pltpu.VMEM((rows, hidden_n), BF16),
@@ -351,7 +378,7 @@
             pltpu.VMEM((n - 1, 1, 2 * LANES), F32),
             pltpu.VMEM((1, 2 * LANES), F32),
             pltpu.VMEM((owners, 1, 2 * LANES), F32),
-            pltpu.SemaphoreType.DMA,
+            pltpu.SemaphoreType.DMA((6,)),
             pltpu.SemaphoreType.DMA((2,)),
             pltpu.SemaphoreType.DMA((2,)),
             pltpu.SemaphoreType.DMA((5,)),
@@ -359,10 +386,16 @@
         ],
         compiler_params=pltpu.CompilerParams(
             collective_id=0, has_side_effects=True, vmem_limit_bytes=60 * 1024 * 1024),
-    )(state_feats.reshape(rows, feat), achieved.reshape(rows, goal_w), offsets.reshape(1, rows),
-      w_in, b_in.reshape(1, hidden_n), w_out.reshape(1, hidden_n), b_out.reshape(1, 1))
-    err, gw, gb, gwo, gbo = out
-    return (err.reshape(ep_dev, steps), gw, gb.reshape(hidden_n), gwo.reshape(hidden_n), gbo.reshape(1))
+    )(state_feats, achieved, offsets.T,
+      w_in, b_in.reshape(1, hidden_n), w_out.reshape(1, hidden_n), b_out)
+    err, gw, gb, gwo, gbo = pl.pallas_call(
+        settle,
+        out_shape=tuple(jax.ShapeDtypeStruct(o.shape, o.dtype) for o in out),
+        in_specs=[vmem] * 5,
+        out_specs=[vmem] * 5,
+        compiler_params=pltpu.CompilerParams(vmem_limit_bytes=4 * 1024 * 1024),
+    )(*out)
+    return (err.T, gw, gb.reshape(hidden_n), gwo.reshape(hidden_n), gbo.reshape(1))
 
 
 def solution(mesh):

time: 78.7 us -> 68.6 us (0.87)
  local copies, waits for them, and re-layouts: 10.2 us -> 2.99 us
  between operations: 3.04 us -> 1.3 us
  other arithmetic: 1.32 us -> 0 us
    reshape x4 -> x0, local copies, waits for them, and re-layouts: 4.07 us -> none  [the longest x1 1.71 us: body(): achieved.reshape(rows, goal_w)]
    unnamed x5 -> x8, local copies, waits for them, and re-layouts: 5.63 us -> 2.99 us
    pallas_call x1 -> x0, other arithmetic: 1.32 us -> none  [body(): pl.pallas_call(functools.partial(kernel, (tm_n, dp_n, steps, rdev, rpad))...]
    pallas_call x0 -> x1, Pallas kernels: none -> 1.25 us  [body(): pl.pallas_call(settle, out_shape=tuple((jax.ShapeDtypeStruct(o.shape, o.d...]
    pallas_call x1, Pallas kernels: 63.7 us -> 62.7 us  [body(): pl.pallas_call(functools.partial(kernel, (tm_n, dp_n, steps, rdev, rpad))...]
where the time goes in v2:
time: 68.6 us; the launch traced here: 68.3 us
  Pallas kernels  64 us (93%)
  local copies, waits for them, and re-layouts  2.99 us (4%)
  between operations  1.3 us (2%)
    pallas_call x1, Pallas kernels, body(): pl.pallas_call(functools.partial(kernel, (tm_n, dp_n, steps, rdev, rpad))...  62.7 us
    unnamed x8, local copies, waits for them, and re-layouts  2.99 us

profile of v2, /device:TPU:0, one launch (start us, length us, event | category | flops | bytes accessed | tf_op | source)
XLA Modules:
  0.0 68.3 jit_solution(11056559909080372402)
XLA Ops:
  1.3 62.7 %shard_map.110 = (f32[4,64]{1,0:T(4,128)}, f32[24,2048]{1,0:T(8,128)}, f32[1,2048]{1,0:T(1,128)}, f32[1,2048]{1,0:T(1,128)}, f32[1,1]{1,0:T(1,128)}) custom-call(bf16[64,4,256]{2,1,0:T(4,128)(2,1)} %sf_hbm.1, bf16[64,4,512]{2,1,0:T(4,128)(2,1)} %ach_hbm.1, s32[4,64]{1,0:T(4,128)} %bitcast.9, bf16[768,2048]{1,0:T(8,128)(2,1)} %w_hbm.1, f32[1,2048]{1,0:T(1,128)} %bitcast.7, ...), custom_call_target="tpu_custom_call" | custom-call | tf_op jit(solution)/shard_map/pallas_call | solution.py:347
  64.0 0.0 copy-start
  64.0 0.9 %copy-done = f32[24,2048]{1,0:T(8,128)S(1)} copy-done((f32[24,2048]{1,0:T(8,128)S(1)}, f32[24,2048]{1,0:T(8,128)}, u32[]{:S(2)}) %copy-start) | copy-done | bytes 196632
  64.9 0.0 copy-start.1
  64.9 0.7 %copy-done.1 = f32[1,2048]{1,0:T(1,128)S(1)} copy-done((f32[1,2048]{1,0:T(1,128)S(1)}, f32[1,2048]{1,0:T(1,128)}, u32[]{:S(2)}) %copy-start.1) | copy-done | bytes 8216
  65.6 0.0 copy-start.2
  65.6 0.7 %copy-done.2 = f32[1,2048]{1,0:T(1,128)S(1)} copy-done((f32[1,2048]{1,0:T(1,128)S(1)}, f32[1,2048]{1,0:T(1,128)}, u32[]{:S(2)}) %copy-start.2) | copy-done | bytes 8216
  66.3 0.0 copy-start.3
  66.3 0.7 copy-done.3
  67.0 1.3 %shard_map.111 = (f32[4,64]{1,0:T(4,128)}, f32[24,2048]{1,0:T(8,128)}, f32[1,2048]{1,0:T(1,128)}, f32[1,2048]{1,0:T(1,128)}, f32[1,1]{1,0:T(1,128)}) custom-call(f32[4,64]{1,0:T(4,128)S(1)} %copy-done.3, f32[24,2048]{1,0:T(8,128)S(1)} %copy-done, f32[1,2048]{1,0:T(1,128)S(1)} %copy-done.1, f32[1,2048]{1,0:T(1,128)S(1)} %copy-done.2, ...), custom_call_target="tpu_custom_call" | custom-call | tf_op jit(solution)/shard_map/pallas_call | solution.py:391
Async XLA Ops:
  64.0 0.9 %copy-start = (f32[24,2048]{1,0:T(8,128)S(1)}, f32[24,2048]{1,0:T(8,128)}, u32[]{:S(2)}) copy-start(f32[24,2048]{1,0:T(8,128)} %get-tuple-element.16.refs_1_) | copy-start | bytes 589828
  64.9 0.7 %copy-start.1 = (f32[1,2048]{1,0:T(1,128)S(1)}, f32[1,2048]{1,0:T(1,128)}, u32[]{:S(2)}) copy-start(f32[1,2048]{1,0:T(1,128)} %get-tuple-element.17.refs_2_) | copy-start | bytes 24580
  65.6 0.7 %copy-start.2 = (f32[1,2048]{1,0:T(1,128)S(1)}, f32[1,2048]{1,0:T(1,128)}, u32[]{:S(2)}) copy-start(f32[1,2048]{1,0:T(1,128)} %get-tuple-element.18.refs_3_) | copy-start | bytes 24580
  66.3 0.7 copy-start.3

commit v3 on v2

--- a/solution.py
+++ b/solution.py
@@ -10,7 +10,6 @@
 
 CAP = 4
 LANES = 128
-GROUP = 8
 MESH = pl.DeviceIdType.MESH
 BF16 = jnp.bfloat16
 F32 = jnp.float32
@@ -39,9 +38,10 @@
 def kernel(dims, sf_hbm, ach_hbm, off_hbm, w_hbm, b_hbm, wo_hbm, bo_ref,
            err_ref, gw_ref, gb_ref, gwo_ref, gbo_ref,
            sf_ref, ach_ref, off_ref, b_ref, wo_ref, w, pre, hid, low, low_send, xt, req_send, req_recv, resp_send, resp_recv,
-           big_send, big_recv, own, sm_send, sm_recv, all_send, all_recv,
-           in_sem, pair_send, pair_recv, s_sem, r_sem):
-    tm_n, dp_n, steps, rdev, rpad = dims
+           near_send, near_recv, far_send, far_recv, mine, sm_send, sm_recv, all_send, all_recv,
+           in_sem, pair_send, pair_recv, s_sem, r_sem, near_sem):
+    tm_n, dp_n, gsz, steps, rdev, rpad = dims
+    groups = tm_n // gsz
     n = tm_n * dp_n
     ep_dev, _, feat = sf_ref.shape
     rows = ep_dev * steps
@@ -226,28 +226,29 @@
     x_copy.wait_recv()
     l_copy.wait_recv()
 
-    block = GROUP * rpad
-    groups = n // GROUP
-
-    def form(g, c):
-        base = lax.rem(me // GROUP + 1 + g, groups)
+    block = gsz * dp_n * rpad
+    outer, place_in = tm // gsz, lax.rem(tm, gsz)
+
+    def form(j, c):
+        base = lax.rem(outer + 1 + j, groups)
         at = pl.ds(pl.multiple_of(base * block, block), block)
         p = dot(xt[0, at, :], low[0]) + dot(xt[1, at, :], low[1])
-        for d in range(GROUP):
-            dev = base * GROUP + d
-            blk = p[d * rpad:(d + 1) * rpad]
-            blk = jnp.concatenate([blk[:, :half // 2], blk[:, half // 2:]], axis=0)
-            big_send[dev] = blk.astype(BF16)
-
-            @pl.when(dev == me)
+        for t in range(gsz):
+            blk = p[t * dp_n * rpad:(t + 1) * dp_n * rpad]
+            blk = jnp.concatenate(
+                [blk[d * rpad:(d + 1) * rpad, z * (half // 2):(z + 1) * (half // 2)]
+                 for d in range(dp_n) for z in range(2)], axis=0)
+
+            @pl.when(place_in == t)
             def _():
-                own[...] = blk
-
-            @pl.when(dev != me)
+                mine[j] = blk
+
+            @pl.when(place_in != t)
             def _():
-                k = lax.rem(dev - me + n, n)
-                remote(big_send.at[dev], big_recv.at[k - 1], s_sem.at[3], r_sem.at[3],
-                       (dev // dp_n, lax.rem(dev, dp_n))).start()
+                k = lax.rem(t - place_in + gsz, gsz)
+                near_send[j, k - 1] = blk.astype(BF16)
+                remote(near_send.at[j, k - 1], near_recv.at[j, k - 1], s_sem.at[3], near_sem.at[j],
+                       (outer * gsz + t, dp)).start()
         return c
 
     lax.fori_loop(0, groups, form, 0)
@@ -267,45 +268,60 @@
 
     if owners == n:
         total()
-        wait_bytes(all_recv.at[pl.ds(0, n - 1)], r_sem.at[4])
     else:
         pl.when(me < owners)(total)
 
-        @pl.when(me < owners)
-        def _():
-            wait_bytes(all_recv.at[pl.ds(0, owners - 1)], r_sem.at[4])
-
-        @pl.when(me >= owners)
-        def _():
-            wait_bytes(all_recv.at[pl.ds(0, owners)], r_sem.at[4])
-    for q in range(hv):
-        lanes = slice(q * LANES, (q + 1) * LANES)
-        gb_ref[:, lanes] = all_recv[q][:, :LANES]
-        gwo_ref[:, lanes] = all_recv[hv + q][:, :LANES]
-    gbo_ref[...] = all_recv[0][:, LANES:LANES + 1]
-
-    wait_bytes(big_recv, r_sem.at[3])
-
-    def add(k, c):
-        same, other = c
-        return same + big_recv[2 * k + 1].astype(F32), other + big_recv[2 * k].astype(F32)
-
-    q4 = half // 4
-    for q in range(2):
-        lanes = slice(q * q4, (q + 1) * q4)
-
-        def add(k, c):
-            same, other = c
-            return (same + big_recv[2 * k + 1, :, lanes].astype(F32),
-                    other + big_recv[2 * k, :, lanes].astype(F32))
-
-        same, other = lax.fori_loop(
-            0, tm_n - 1, add, (own[:, lanes], jnp.zeros((2 * rpad, q4), F32)))
-        other = other + big_recv[n - 2, :, lanes].astype(F32)
-        for which, val in ((dp, same), (1 - dp, other)):
-            for z in range(2):
-                col = pl.multiple_of(which * half + z * (half // 2) + q * q4, LANES)
-                gw_ref[:, pl.ds(col, q4)] = val[z * rpad:z * rpad + rdev]
+    def small_out():
+        if owners == n:
+            wait_bytes(all_recv.at[pl.ds(0, n - 1)], r_sem.at[4])
+        else:
+            @pl.when(me < owners)
+            def _():
+                wait_bytes(all_recv.at[pl.ds(0, owners - 1)], r_sem.at[4])
+
+            @pl.when(me >= owners)
+            def _():
+                wait_bytes(all_recv.at[pl.ds(0, owners)], r_sem.at[4])
+        for q in range(hv):
+            lanes = slice(q * LANES, (q + 1) * LANES)
+            gb_ref[:, lanes] = all_recv[q][:, :LANES]
+            gwo_ref[:, lanes] = all_recv[hv + q][:, :LANES]
+        gbo_ref[...] = all_recv[0][:, LANES:LANES + 1]
+
+    def gathered(j, rows_at, nrows):
+        tot = mine[j, pl.ds(rows_at, nrows), :]
+        for k in range(gsz - 1):
+            tot = tot + near_recv[j, k, pl.ds(rows_at, nrows), :].astype(F32)
+        return tot
+
+    def forward(j, c):
+        wait_bytes(near_recv.at[j], near_sem.at[j])
+        to = lax.rem(outer + 1 + j, groups) * gsz + place_in
+        for d in range(dp_n):
+            far_send[j, d] = gathered(j, d * 2 * rpad, 2 * rpad).astype(BF16)
+            remote(far_send.at[j, d], far_recv.at[dp_n * j + lax.rem(dp + d, dp_n)], s_sem.at[5], r_sem.at[3],
+                   (to, d)).start()
+        return c
+
+    last = groups - 1
+    lax.fori_loop(0, last, forward, 0)
+    wait_bytes(near_recv.at[last], near_sem.at[last])
+    far_send[last, 0] = gathered(last, pl.multiple_of((1 - dp) * 2 * rpad, 2 * rpad), 2 * rpad).astype(BF16)
+    cross = remote(far_send.at[last, 0], far_recv.at[dp_n * last], pair_send.at[2], pair_recv.at[2], partner)
+    cross.start()
+    same = gathered(last, pl.multiple_of(dp * 2 * rpad, 2 * rpad), 2 * rpad)
+    small_out()
+    wait_bytes(far_recv.at[pl.ds(0, dp_n * last)], r_sem.at[3])
+    other = jnp.zeros((2 * rpad, half // 2), F32)
+    for j in range(last):
+        same = same + far_recv[dp_n * j].astype(F32)
+        other = other + far_recv[dp_n * j + 1].astype(F32)
+    cross.wait_recv()
+    other = other + far_recv[dp_n * last].astype(F32)
+    for which, val in ((dp, same), (1 - dp, other)):
+        for z in range(2):
+            col = pl.multiple_of(which * half + z * (half // 2), LANES)
+            gw_ref[:, pl.ds(col, half // 2)] = val[z * rpad:z * rpad + rdev]
 
     wait_bytes(req_send, s_sem.at[0])
     wait_bytes(resp_send, s_sem.at[1])
@@ -323,7 +339,9 @@
         @pl.when(me >= owners)
         def _():
             wait_bytes(sm_send.at[pl.ds(0, owners)], s_sem.at[2])
-    wait_bytes(big_send.at[pl.ds(0, n - 1)], s_sem.at[3])
+    wait_bytes(near_send, s_sem.at[3])
+    wait_bytes(far_send.at[pl.ds(0, last)], s_sem.at[5])
+    cross.wait_send()
 
 
 def settle(*refs):
@@ -342,10 +360,13 @@
     rpad = -(-rdev // 8) * 8
     slots = CAP * (goal_w // LANES)
     owners = 2 * hidden_n // LANES
-    assert dp_n == 2 and rows <= 256 and owners <= n and n % GROUP == 0
+    gsz = 2 ** (int(math.log2(tm_n)) // 2)
+    groups = tm_n // gsz
+    piece = 2 * dp_n * rpad
+    assert dp_n == 2 and rows <= 256 and owners <= n and tm_n % gsz == 0
     vmem = pl.BlockSpec(memory_space=pltpu.VMEM)
     out = pl.pallas_call(
-        functools.partial(kernel, (tm_n, dp_n, steps, rdev, rpad)),
+        functools.partial(kernel, (tm_n, dp_n, gsz, steps, rdev, rpad)),
         out_shape=(
             jax.ShapeDtypeStruct((steps, ep_dev), F32),
             jax.ShapeDtypeStruct((rdev, hidden_n), F32),
@@ -371,18 +392,21 @@
             pltpu.VMEM((tm_n - 1, slots, LANES), BF16),
             pltpu.VMEM((tm_n - 1, slots, LANES), BF16),
             pltpu.VMEM((tm_n - 1, slots, LANES), BF16),
-            pltpu.VMEM((n, 2 * rpad, half // 2), BF16),
-            pltpu.VMEM((n - 1, 2 * rpad, half // 2), BF16),
-            pltpu.VMEM((2 * rpad, half // 2), F32),
+            pltpu.VMEM((groups, gsz - 1, piece, half // 2), BF16),
+            pltpu.VMEM((groups, gsz - 1, piece, half // 2), BF16),
+            pltpu.VMEM((groups, dp_n, 2 * rpad, half // 2), BF16),
+            pltpu.VMEM((dp_n * (groups - 1) + 1, 2 * rpad, half // 2), BF16),
+            pltpu.VMEM((groups, piece, half // 2), F32),
             pltpu.VMEM((owners, 1, 2 * LANES), F32),
             pltpu.VMEM((n - 1, 1, 2 * LANES), F32),
             pltpu.VMEM((1, 2 * LANES), F32),
             pltpu.VMEM((owners, 1, 2 * LANES), F32),
             pltpu.SemaphoreType.DMA((6,)),
-            pltpu.SemaphoreType.DMA((2,)),
-            pltpu.SemaphoreType.DMA((2,)),
+            pltpu.SemaphoreType.DMA((3,)),
+            pltpu.SemaphoreType.DMA((3,)),
+            pltpu.SemaphoreType.DMA((6,)),
             pltpu.SemaphoreType.DMA((5,)),
-            pltpu.SemaphoreType.DMA((5,)),
+            pltpu.SemaphoreType.DMA((groups,)),
         ],
         compiler_params=pltpu.CompilerParams(
             collective_id=0, has_side_effects=True, vmem_limit_bytes=60 * 1024 * 1024),
@@ -393,7 +417,7 @@
         out_shape=tuple(jax.ShapeDtypeStruct(o.shape, o.dtype) for o in out),
         in_specs=[vmem] * 5,
         out_specs=[vmem] * 5,
-        compiler_params=pltpu.CompilerParams(vmem_limit_bytes=4 * 1024 * 1024),
+        compiler_params=pltpu.CompilerParams(vmem_limit_bytes=60 * 1024 * 1024),
     )(*out)
     return (err.T, gw, gb.reshape(hidden_n), gwo.reshape(hidden_n), gbo.reshape(1))
 

time: 68.6 us -> 47 us (0.69)
  Pallas kernels: 64 us -> 45.5 us
  local copies, waits for them, and re-layouts: 2.99 us -> 0 us
    pallas_call x1, Pallas kernels: 62.7 us -> 43.3 us  [body(): pl.pallas_call(functools.partial(kernel, (tm_n, dp_n, gsz, steps, rdev, r...]
    unnamed x8 -> x0, local copies, waits for them, and re-layouts: 2.99 us -> none
    pallas_call x1, Pallas kernels: 1.25 us -> 2.26 us  [body(): pl.pallas_call(settle, out_shape=tuple((jax.ShapeDtypeStruct(o.shape, o.d...]
where the time goes in v3:
time: 47 us; the launch traced here: 46.8 us
  Pallas kernels  45.5 us (97%)
  between operations  1.29 us (3%)
    pallas_call x1, Pallas kernels, body(): pl.pallas_call(functools.partial(kernel, (tm_n, dp_n, gsz, steps, rdev, r...  43.3 us
    pallas_call x1, Pallas kernels, body(): pl.pallas_call(settle, out_shape=tuple((jax.ShapeDtypeStruct(o.shape, o.d...  2.26 us

profile of v3, /device:TPU:0, one launch (start us, length us, event | category | flops | bytes accessed | tf_op | source)
XLA Modules:
  0.0 46.8 jit_solution(8345327615325672774)
XLA Ops:
  1.3 43.3 %shard_map.110 = (f32[4,64]{1,0:T(4,128)}, f32[24,2048]{1,0:T(8,128)}, f32[1,2048]{1,0:T(1,128)}, f32[1,2048]{1,0:T(1,128)}, f32[1,1]{1,0:T(1,128)}) custom-call(bf16[64,4,256]{2,1,0:T(4,128)(2,1)} %sf_hbm.1, bf16[64,4,512]{2,1,0:T(4,128)(2,1)} %ach_hbm.1, s32[4,64]{1,0:T(4,128)} %bitcast.9, bf16[768,2048]{1,0:T(8,128)(2,1)} %w_hbm.1, f32[1,2048]{1,0:T(1,128)} %bitcast.7, ...), custom_call_target="tpu_custom_call" | custom-call | tf_op jit(solution)/shard_map/pallas_call | solution.py:368
  44.5 2.3 %shard_map.111 = (f32[4,64]{1,0:T(4,128)}, f32[24,2048]{1,0:T(8,128)}, f32[1,2048]{1,0:T(1,128)}, f32[1,2048]{1,0:T(1,128)}, f32[1,1]{1,0:T(1,128)}) custom-call(f32[4,64]{1,0:T(4,128)} %get-tuple-element.15.refs_0_, f32[24,2048]{1,0:T(8,128)} %get-tuple-element.16.refs_1_, f32[1,2048]{1,0:T(1,128)} %get-tuple-element.17.refs_2_, ...), custom_call_target="tpu_custom_call" | custom-call | tf_op jit(solution)/shard_map/pallas_call | solution.py:415

commit v4 on v3

--- a/solution.py
+++ b/solution.py
@@ -38,8 +38,8 @@
 def kernel(dims, sf_hbm, ach_hbm, off_hbm, w_hbm, b_hbm, wo_hbm, bo_ref,
            err_ref, gw_ref, gb_ref, gwo_ref, gbo_ref,
            sf_ref, ach_ref, off_ref, b_ref, wo_ref, w, pre, hid, low, low_send, xt, req_send, req_recv, resp_send, resp_recv,
-           near_send, near_recv, far_send, far_recv, mine, sm_send, sm_recv, all_send, all_recv,
-           in_sem, pair_send, pair_recv, s_sem, r_sem, near_sem):
+           near_send, near_recv, mid_send, mid_recv, far_send, far_recv, mine, sm_send, sm_recv, all_send, all_recv,
+           in_sem, pair_send, pair_recv, s_sem, r_sem, near_sem, mid_sem):
     tm_n, dp_n, gsz, steps, rdev, rpad = dims
     groups = tm_n // gsz
     n = tm_n * dp_n
@@ -228,6 +228,10 @@
 
     block = gsz * dp_n * rpad
     outer, place_in = tm // gsz, lax.rem(tm, gsz)
+    flip_low = place_in + 1 - 2 * lax.rem(place_in, 2)
+    flip_high = place_in + 2 - 4 * (place_in // 2)
+    first_hop = flip_low * (1 - dp) + flip_high * dp
+    second_hop = flip_high * (1 - dp) + flip_low * dp
 
     def form(j, c):
         base = lax.rem(outer + 1 + j, groups)
@@ -241,14 +245,21 @@
 
             @pl.when(place_in == t)
             def _():
-                mine[j] = blk
-
-            @pl.when(place_in != t)
-            def _():
-                k = lax.rem(t - place_in + gsz, gsz)
-                near_send[j, k - 1] = blk.astype(BF16)
-                remote(near_send.at[j, k - 1], near_recv.at[j, k - 1], s_sem.at[3], near_sem.at[j],
-                       (outer * gsz + t, dp)).start()
+                mine[j, 0] = blk
+
+            @pl.when(second_hop == t)
+            def _():
+                mine[j, 1] = blk
+
+            @pl.when(first_hop == t)
+            def _():
+                near_send[j, 0] = blk.astype(BF16)
+
+            @pl.when(gsz - 1 - place_in == t)
+            def _():
+                near_send[j, 1] = blk.astype(BF16)
+        remote(near_send.at[j], near_recv.at[j], s_sem.at[3], near_sem.at[j],
+               (outer * gsz + first_hop, dp)).start()
         return c
 
     lax.fori_loop(0, groups, form, 0)
@@ -289,13 +300,18 @@
         gbo_ref[...] = all_recv[0][:, LANES:LANES + 1]
 
     def gathered(j, rows_at, nrows):
-        tot = mine[j, pl.ds(rows_at, nrows), :]
-        for k in range(gsz - 1):
-            tot = tot + near_recv[j, k, pl.ds(rows_at, nrows), :].astype(F32)
-        return tot
+        at = pl.ds(rows_at, nrows)
+        return mine[j, 0, at, :] + near_recv[j, 0, at, :].astype(F32) + mid_recv[j, at, :].astype(F32)
+
+    def relay(j):
+        wait_bytes(near_recv.at[j], near_sem.at[j])
+        mid_send[j] = (mine[j, 1] + near_recv[j, 1].astype(F32)).astype(BF16)
+        remote(mid_send.at[j], mid_recv.at[j], s_sem.at[6], mid_sem.at[j],
+               (outer * gsz + second_hop, dp)).start()
 
     def forward(j, c):
-        wait_bytes(near_recv.at[j], near_sem.at[j])
+        relay(j + 1)
+        wait_bytes(mid_recv.at[j], mid_sem.at[j])
         to = lax.rem(outer + 1 + j, groups) * gsz + place_in
         for d in range(dp_n):
             far_send[j, d] = gathered(j, d * 2 * rpad, 2 * rpad).astype(BF16)
@@ -304,8 +320,9 @@
         return c
 
     last = groups - 1
+    relay(0)
     lax.fori_loop(0, last, forward, 0)
-    wait_bytes(near_recv.at[last], near_sem.at[last])
+    wait_bytes(mid_recv.at[last], mid_sem.at[last])
     far_send[last, 0] = gathered(last, pl.multiple_of((1 - dp) * 2 * rpad, 2 * rpad), 2 * rpad).astype(BF16)
     cross = remote(far_send.at[last, 0], far_recv.at[dp_n * last], pair_send.at[2], pair_recv.at[2], partner)
     cross.start()
@@ -340,6 +357,7 @@
         def _():
             wait_bytes(sm_send.at[pl.ds(0, owners)], s_sem.at[2])
     wait_bytes(near_send, s_sem.at[3])
+    wait_bytes(mid_send, s_sem.at[6])
     wait_bytes(far_send.at[pl.ds(0, last)], s_sem.at[5])
     cross.wait_send()
 
@@ -360,7 +378,7 @@
     rpad = -(-rdev // 8) * 8
     slots = CAP * (goal_w // LANES)
     owners = 2 * hidden_n // LANES
-    gsz = 2 ** (int(math.log2(tm_n)) // 2)
+    gsz = 4
     groups = tm_n // gsz
     piece = 2 * dp_n * rpad
     assert dp_n == 2 and rows <= 256 and owners <= n and tm_n % gsz == 0
@@ -392,11 +410,13 @@
             pltpu.VMEM((tm_n - 1, slots, LANES), BF16),
             pltpu.VMEM((tm_n - 1, slots, LANES), BF16),
             pltpu.VMEM((tm_n - 1, slots, LANES), BF16),
-            pltpu.VMEM((groups, gsz - 1, piece, half // 2), BF16),
-            pltpu.VMEM((groups, gsz - 1, piece, half // 2), BF16),
+            pltpu.VMEM((groups, 2, piece, half // 2), BF16),
+            pltpu.VMEM((groups, 2, piece, half // 2), BF16),
+            pltpu.VMEM((groups, piece, half // 2), BF16),
+            pltpu.VMEM((groups, piece, half // 2), BF16),
             pltpu.VMEM((groups, dp_n, 2 * rpad, half // 2), BF16),
             pltpu.VMEM((dp_n * (groups - 1) + 1, 2 * rpad, half // 2), BF16),
-            pltpu.VMEM((groups, piece, half // 2), F32),
+            pltpu.VMEM((groups, 2, piece, half // 2), F32),
             pltpu.VMEM((owners, 1, 2 * LANES), F32),
             pltpu.VMEM((n - 1, 1, 2 * LANES), F32),
             pltpu.VMEM((1, 2 * LANES), F32),
@@ -404,8 +424,9 @@
             pltpu.SemaphoreType.DMA((6,)),
             pltpu.SemaphoreType.DMA((3,)),
             pltpu.SemaphoreType.DMA((3,)),
-            pltpu.SemaphoreType.DMA((6,)),
+            pltpu.SemaphoreType.DMA((7,)),
             pltpu.SemaphoreType.DMA((5,)),
+            pltpu.SemaphoreType.DMA((groups,)),
             pltpu.SemaphoreType.DMA((groups,)),
         ],
         compiler_params=pltpu.CompilerParams(

time: 47 us -> 45.9 us (0.977)
  Pallas kernels: 45.5 us -> 44.2 us
    pallas_call x1, Pallas kernels: 43.3 us -> 41.9 us  [body(): pl.pallas_call(functools.partial(kernel, (tm_n, dp_n, gsz, steps, rdev, r...]
where the time goes in v4:
time: 45.9 us; the launch traced here: 45.4 us
  Pallas kernels  44.2 us (96%)
  between operations  1.29 us (3%)
    pallas_call x1, Pallas kernels, body(): pl.pallas_call(functools.partial(kernel, (tm_n, dp_n, gsz, steps, rdev, r...  41.9 us
    pallas_call x1, Pallas kernels, body(): pl.pallas_call(settle, out_shape=tuple((jax.ShapeDtypeStruct(o.shape, o.d...  2.26 us

profile of v4, /device:TPU:0, one launch (start us, length us, event | category | flops | bytes accessed | tf_op | source)
XLA Modules:
  0.0 45.4 jit_solution(397911983267334385)
XLA Ops:
  1.3 41.9 %shard_map.110 = (f32[4,64]{1,0:T(4,128)}, f32[24,2048]{1,0:T(8,128)}, f32[1,2048]{1,0:T(1,128)}, f32[1,2048]{1,0:T(1,128)}, f32[1,1]{1,0:T(1,128)}) custom-call(bf16[64,4,256]{2,1,0:T(4,128)(2,1)} %sf_hbm.1, bf16[64,4,512]{2,1,0:T(4,128)(2,1)} %ach_hbm.1, s32[4,64]{1,0:T(4,128)} %bitcast.9, bf16[768,2048]{1,0:T(8,128)(2,1)} %w_hbm.1, f32[1,2048]{1,0:T(1,128)} %bitcast.7, ...), custom_call_target="tpu_custom_call" | custom-call | tf_op jit(solution)/shard_map/pallas_call | solution.py:386
  43.2 2.3 %shard_map.111 = (f32[4,64]{1,0:T(4,128)}, f32[24,2048]{1,0:T(8,128)}, f32[1,2048]{1,0:T(1,128)}, f32[1,2048]{1,0:T(1,128)}, f32[1,1]{1,0:T(1,128)}) custom-call(f32[4,64]{1,0:T(4,128)} %get-tuple-element.15.refs_0_, f32[24,2048]{1,0:T(8,128)} %get-tuple-element.16.refs_1_, f32[1,2048]{1,0:T(1,128)} %get-tuple-element.17.refs_2_, ...), custom_call_target="tpu_custom_call" | custom-call | tf_op jit(solution)/shard_map/pallas_call | solution.py:436

commit v5 on v4

--- a/solution.py
+++ b/solution.py
@@ -277,11 +277,6 @@
 
         lax.fori_loop(1, n, tell, 0)
 
-    if owners == n:
-        total()
-    else:
-        pl.when(me < owners)(total)
-
     def small_out():
         if owners == n:
             wait_bytes(all_recv.at[pl.ds(0, n - 1)], r_sem.at[4])
@@ -321,7 +316,12 @@
 
     last = groups - 1
     relay(0)
-    lax.fori_loop(0, last, forward, 0)
+    lax.fori_loop(0, 1, forward, 0)
+    if owners == n:
+        total()
+    else:
+        pl.when(me < owners)(total)
+    lax.fori_loop(1, last, forward, 0)
     wait_bytes(mid_recv.at[last], mid_sem.at[last])
     far_send[last, 0] = gathered(last, pl.multiple_of((1 - dp) * 2 * rpad, 2 * rpad), 2 * rpad).astype(BF16)
     cross = remote(far_send.at[last, 0], far_recv.at[dp_n * last], pair_send.at[2], pair_recv.at[2], partner)

time: 45.9 us -> 45.3 us (0.987)
  Pallas kernels: 44.2 us -> 43.6 us
    pallas_call x1, Pallas kernels: 41.9 us -> 41.3 us  [body(): pl.pallas_call(functools.partial(kernel, (tm_n, dp_n, gsz, steps, rdev, r...]
where the time goes in v5:
time: 45.3 us; the launch traced here: 44.9 us
  Pallas kernels  43.6 us (96%)
  between operations  1.29 us (3%)
    pallas_call x1, Pallas kernels, body(): pl.pallas_call(functools.partial(kernel, (tm_n, dp_n, gsz, steps, rdev, r...  41.3 us
    pallas_call x1, Pallas kernels, body(): pl.pallas_call(settle, out_shape=tuple((jax.ShapeDtypeStruct(o.shape, o.d...  2.26 us

profile of v5, /device:TPU:0, one launch (start us, length us, event | category | flops | bytes accessed | tf_op | source)
XLA Modules:
  0.0 44.9 jit_solution(6548924271283082135)
XLA Ops:
  1.3 41.3 %shard_map.110 = (f32[4,64]{1,0:T(4,128)}, f32[24,2048]{1,0:T(8,128)}, f32[1,2048]{1,0:T(1,128)}, f32[1,2048]{1,0:T(1,128)}, f32[1,1]{1,0:T(1,128)}) custom-call(bf16[64,4,256]{2,1,0:T(4,128)(2,1)} %sf_hbm.1, bf16[64,4,512]{2,1,0:T(4,128)(2,1)} %ach_hbm.1, s32[4,64]{1,0:T(4,128)} %bitcast.9, bf16[768,2048]{1,0:T(8,128)(2,1)} %w_hbm.1, f32[1,2048]{1,0:T(1,128)} %bitcast.7, ...), custom_call_target="tpu_custom_call" | custom-call | tf_op jit(solution)/shard_map/pallas_call | solution.py:386
  42.6 2.3 %shard_map.111 = (f32[4,64]{1,0:T(4,128)}, f32[24,2048]{1,0:T(8,128)}, f32[1,2048]{1,0:T(1,128)}, f32[1,2048]{1,0:T(1,128)}, f32[1,1]{1,0:T(1,128)}) custom-call(f32[4,64]{1,0:T(4,128)} %get-tuple-element.15.refs_0_, f32[24,2048]{1,0:T(8,128)} %get-tuple-element.16.refs_1_, f32[1,2048]{1,0:T(1,128)} %get-tuple-element.17.refs_2_, ...), custom_call_target="tpu_custom_call" | custom-call | tf_op jit(solution)/shard_map/pallas_call | solution.py:436
